TPU v7x, 256 devices: a whole 4x4x8 slice. The times are simulated.
256 devices in a mesh: row: 32 (over x, z_hi, core), col: 8 (over y, z_lo).
Axes of the slice: x: 4, y: 4, z: 8 (z_hi: 4, z_lo: 2; z = z_hi * 2 + z_lo), core: 2. Of those that a mesh axis runs over, the one named last changes fastest.
Arguments:
- sigma_anc: float32 [128, 128, 128, 128], P('row', 'col'), as said below
- panel: float32 [2, 128, 128, 512], P(None, 'row'), may hold values from -0.12 to 0.12
- pattern: int32 [2, 64], replicated, may hold values from 0 to 127, as said below
- linv: float32 [2, 512, 512], replicated, as said below
Outputs:
- sigma_sj: float32 [2, 128, 128, 512], P(None, 'row')
- sigma_jj: float32 [2, 512, 512], replicated
Inputs may be any that keep to these rules, and one draw needn't show every extreme that they name: `pattern`: each row lists 64 distinct ancestor block indices in increasing order; 0 and 127 are always among them. `sigma_anc`: symmetric as a matrix of order 128 * 128 in ancestor order. `linv`: lower triangular, diagonal entries between 1 and 2.
All inputs are finite; a program needn't handle non-finite values.
Results may differ from a plain program's by a relative error of at most 0.0001.
Values sent between devices are 32-bit elements; how exact they have to be, the bound alone decides.
A program may use at most 128 MiB of HBM per device.

v0:
```python
import jax
import jax.numpy as jnp
from jax import lax
from jax.sharding import PartitionSpec as P


def local(sigma_anc, panel, pattern, linv):
    highest = lax.Precision.HIGHEST
    rows_here = sigma_anc.shape[0]
    cols_here = sigma_anc.shape[1]
    row_count = lax.axis_size("row")
    col_count = lax.axis_size("col")
    row_index = lax.axis_index("row")
    column_index = lax.axis_index("col")
    row_ids = jnp.arange(rows_here, dtype=jnp.int32) * row_count + row_index
    col_ids = jnp.arange(cols_here, dtype=jnp.int32) * col_count + column_index
    in_pattern = jnp.any(pattern[:, :, None] == row_ids[None, None, :], axis=1).astype(jnp.float32)
    updated = jnp.einsum(
        "sqiw,swv->sqiv", panel, linv, precision=highest, preferred_element_type=jnp.float32
    )
    updated = updated * in_pattern[:, :, None, None]
    selector = (col_ids[:, None] == row_ids[None, :]).astype(jnp.float32)
    local_cols = jnp.einsum(
        "kq,sqiw->skiw", selector, updated, precision=highest, preferred_element_type=jnp.float32
    )
    gathered_cols = lax.psum(local_cols, "row")
    partial_value = jnp.einsum(
        "qkij,skjw->sqiw",
        sigma_anc,
        gathered_cols,
        precision=highest,
        preferred_element_type=jnp.float32,
    )
    product = lax.psum(partial_value, "col")
    product = product * in_pattern[:, :, None, None]
    sigma_sj = -product
    base_term = jnp.einsum(
        "siw,siv->swv", linv, linv, precision=highest, preferred_element_type=jnp.float32
    )
    local_term = jnp.einsum(
        "sqiw,sqiv->swv", updated, product, precision=highest, preferred_element_type=jnp.float32
    )
    total_term = lax.psum(local_term, "row")
    sigma_jj = base_term + total_term
    return (sigma_sj, sigma_jj)


def solution(mesh):
    return jax.shard_map(
        local,
        mesh=mesh,
        in_specs=(P("row", "col", None, None), P(None, "row", None, None), P(), P()),
        out_specs=(P(None, "row", None, None), P()),
        check_vma=False,
    )
```

profile of v0, /device:TPU:1, one launch (start us, length us, event | category | flops | bytes accessed | tf_op | source)
XLA Modules:
  0.0 793.9 jit_solution(9738361498573340036)
XLA Ops:
  7.2 0.0 copy-start
  7.2 0.0 all-reduce.4.cloned.1.call-start
  7.3 1.0 compare_reduce_fusion
  8.3 0.5 copy-done
  8.8 5.1 fusion.12
  13.9 0.0 copy-start.1
  13.9 1.3 copy-done.1
  15.2 6.0 fusion.5
  21.2 10.0 %copy.15 = f32[2,128,512,16]{1,2,3,0:T(8,128)} copy(f32[2,128,512,16]{2,3,1,0:T(8,128)} %fusion.5) | data formatting | bytes 16777216 | tf_op jit(solution)/shard_map/kq,sqiw->skiw/dot_general | solution.py:23
  31.2 0.0 all-reduce.4.cloned.1.call-update
  31.2 0.2 all-reduce.6.cloned.1.call-start
  31.5 328.1 %all-reduce.4.cloned.1.call-done = f32[2,16,128,512]{2,3,1,0:T(8,128)} async-done(((f32[2,16,128,512]{2,3,1,0:T(8,128)}), f32[2,16,128,512]{2,3,1,0:T(8,128)}) %all-reduce.4.cloned.1.call-update) | async-done | bytes 8388624 | tf_op jit(solution)/shard_map/psum | solution.py:26
  359.6 17.7 %fusion.15 = f32[2,4,128,512]{3,2,1,0:T(8,128)} fusion(f32[4,16,128,128]{3,2,1,0:T(8,128)} %param.4, f32[2,16,128,512]{2,3,1,0:T(8,128)} %all-reduce.4.cloned.1.call-done), kind=kOutput, calls=%fused_computation.12 | convolution fusion | flops 12884901888 | bytes 14680064 | tf_op jit(solution)/shard_map/qkij,skjw->sqiw/dot_general | solution.py:27
  377.3 0.0 all-reduce.6.cloned.1.call-update
  377.4 0.3 all-reduce.8.cloned.1.call-start
  377.6 107.8 %all-reduce.6.cloned.1.call-done = f32[2,4,128,512]{3,2,1,0:T(8,128)} async-done(((f32[2,4,128,512]{3,2,1,0:T(8,128)}), f32[2,4,128,512]{3,2,1,0:T(8,128)}) %all-reduce.6.cloned.1.call-update) | async-done | bytes 2097168 | tf_op jit(solution)/shard_map/psum | solution.py:34
  485.4 7.4 fusion.9
  492.8 0.0 all-reduce.8.cloned.1.call-update
  492.8 3.4 multiply_negate_fusion
  496.2 285.3 %all-reduce.8.cloned.1.call-done = f32[2,512,512]{2,1,0:T(8,128)} async-done(((f32[2,512,512]{2,1,0:T(8,128)}), f32[2,512,512]{2,1,0:T(8,128)}) %all-reduce.8.cloned.1.call-update) | async-done | bytes 2097168 | tf_op jit(solution)/shard_map/psum | solution.py:43
  781.4 5.9 convolution_add_fusion
  (3 shorter events, 0.0 us)
Async XLA Ops:
  7.2 1.6 copy-start
  7.2 352.4 %all-reduce.4.cloned.1.call-start = ((), (), s32[]{:S(2)}) async-start(), calls=%async_computation | async-start | bytes 16777216 | tf_op jit(solution)/shard_map/psum | solution.py:26
  13.9 1.3 copy-start.1
  31.2 454.2 %all-reduce.6.cloned.1.call-start = ((), (), s32[]{:S(2)}) async-start(), calls=%async_computation.1 | async-start | bytes 4194304 | tf_op jit(solution)/shard_map/psum | solution.py:34
  377.4 404.1 %all-reduce.8.cloned.1.call-start = ((), (), s32[]{:S(2)}) async-start(), calls=%async_computation.2 | async-start | bytes 4194304 | tf_op jit(solution)/shard_map/psum | solution.py:43
Sparse Core Ops, SparseCore 0:
  31.4 328.1 all-reduce.3
  377.5 107.8 all-reduce.5
  492.9 288.4 all-reduce.7
where the time goes:
time: 794 us
  waiting for transfers between devices  721 us (91%)
  matrix products  42.1 us (5%)
  between operations  13.8 us (2%)
  local copies, waits for them, and re-layouts  11.9 us (1%)
    psum x1, waiting for transfers between devices, local(): gathered_cols = lax.psum(local_cols, 'row')  328 us
    psum x1, waiting for transfers between devices, local(): total_term = lax.psum(local_term, 'row')  285 us
    psum x1, waiting for transfers between devices, local(): product = lax.psum(partial_value, 'col')  108 us
    dot_general x1, matrix products, local(): jnp.einsum('qkij,skjw->sqiw', sigma_anc, gathered_cols, precision=highest...  17.7 us
  transfers between devices with their start and end apart: 3, of which 3 were waited for; matrix products, arithmetic and copies ran while one was open for 0% of the time, Pallas kernels for 0%

commit v1 on v0

--- a/solution.py
+++ b/solution.py
@@ -40,7 +40,7 @@
     local_term = jnp.einsum(
         "sqiw,sqiv->swv", updated, product, precision=highest, preferred_element_type=jnp.float32
     )
-    total_term = lax.psum(local_term, "row")
+    total_term = jnp.sum(lax.all_gather(local_term, "row"), 0)
     sigma_jj = base_term + total_term
     return (sigma_sj, sigma_jj)
 

time: 794 us -> 894 us (1.13)
  waiting for transfers between devices: 721 us -> 803 us
  other arithmetic: 4.37 us -> 26.6 us
    all_gather x0 -> x1, waiting for transfers between devices: none -> 374 us  [local(): total_term = jnp.sum(lax.all_gather(local_term, 'row'), 0)]
    psum x1 -> x0, waiting for transfers between devices: 285 us -> none  [local(): total_term = lax.psum(local_term, 'row')]
    reduce_sum x0 -> x1, other arithmetic: none -> 22.2 us  [local(): total_term = jnp.sum(lax.all_gather(local_term, 'row'), 0)]
    dot_general x1 -> x0, local copies, waits for them, and re-layouts: 10 us -> none  [local(): jnp.einsum('kq,sqiw->skiw', selector, updated, precision=highest, preferr...]
  transfers between devices with their start and end apart: 3 -> 3, of which waited for: 3 -> 3; matrix products, arithmetic and copies ran while one was open for 0% -> 1% of each run, Pallas kernels for 0% -> 0%
where the time goes in v1:
time: 894 us
  waiting for transfers between devices  803 us (90%)
  matrix products  42.5 us (5%)
  other arithmetic  26.6 us (3%)
  between operations  13.8 us (2%)
    all_gather x1, waiting for transfers between devices, local(): total_term = jnp.sum(lax.all_gather(local_term, 'row'), 0)  374 us
    psum x1, waiting for transfers between devices, local(): gathered_cols = lax.psum(local_cols, 'row')  321 us
    psum x1, waiting for transfers between devices, local(): product = lax.psum(partial_value, 'col')  108 us
    reduce_sum x1, other arithmetic, local(): total_term = jnp.sum(lax.all_gather(local_term, 'row'), 0)  22.2 us
    dot_general x1, matrix products, local(): jnp.einsum('qkij,skjw->sqiw', sigma_anc, gathered_cols, precision=highest...  18 us
  transfers between devices with their start and end apart: 3, of which 3 were waited for; matrix products, arithmetic and copies ran while one was open for 1% of the time, Pallas kernels for 0%

profile of v1, /device:TPU:1, one launch (start us, length us, event | category | flops | bytes accessed | tf_op | source)
XLA Modules:
  0.0 893.8 jit_solution(10784491128204240918)
XLA Ops:
  7.2 0.0 copy-start
  7.2 0.0 all-reduce.3.cloned.1.call-start
  7.3 1.0 compare_reduce_fusion
  8.3 0.5 copy-done
  8.8 5.1 fusion.13
  13.9 0.0 copy-start.1
  13.9 1.3 copy-done.1
  15.2 6.1 convolution_bitcast_fusion
  21.3 0.0 all-reduce.3.cloned.1.call-update
  21.3 0.2 all-reduce.5.cloned.1.call-start
  21.6 5.4 copy.20
  27.0 321.5 %all-reduce.3.cloned.1.call-done = f32[2,16,128,512]{3,1,2,0:T(8,128)} async-done(((f32[2,16,128,512]{3,1,2,0:T(8,128)}), f32[2,16,128,512]{3,1,2,0:T(8,128)}) %all-reduce.3.cloned.1.call-update) | async-done | bytes 8388624 | tf_op jit(solution)/shard_map/psum | solution.py:26
  348.5 18.0 %fusion.7 = f32[2,4,128,512]{3,2,1,0:T(8,128)} fusion(f32[4,16,128,128,1]{2,1,3,0,4:T(8,128)} %copy.20, f32[2,16,128,512]{3,1,2,0:T(8,128)} %all-reduce.3.cloned.1.call-done), kind=kOutput, calls=%fused_computation.9 | convolution fusion | flops 12884901888 | bytes 14680064 | tf_op jit(solution)/shard_map/qkij,skjw->sqiw/dot_general | solution.py:27
  366.5 0.0 all-reduce.5.cloned.1.call-update
  366.5 0.3 all-gather.3.cloned.1.call-start
  366.8 107.8 %all-reduce.5.cloned.1.call-done = f32[2,4,128,512]{3,2,1,0:T(8,128)} async-done(((f32[2,4,128,512]{3,2,1,0:T(8,128)}), f32[2,4,128,512]{3,2,1,0:T(8,128)}) %all-reduce.5.cloned.1.call-update) | async-done | bytes 2097168 | tf_op jit(solution)/shard_map/psum | solution.py:34
  474.6 7.4 fusion.10
  481.9 0.0 all-gather.3.cloned.1.call-update
  482.0 3.4 multiply_negate_fusion
  485.3 373.8 %all-gather.3.cloned.1.call-done = f32[64,512,512]{2,1,0:T(8,128)} async-done(((f32[2,512,512]{2,1,0:T(8,128)}), f32[64,512,512]{2,1,0:T(8,128)}) %all-gather.3.cloned.1.call-update) | async-done | bytes 67108880 | tf_op jit(solution)/shard_map/all_gather | solution.py:43
  859.1 22.2 %reduce_sum.9 = f32[2,512,512]{2,1,0:T(8,128)} reduce(f32[32,2,512,512]{3,2,1,0:T(8,128)} %bitcast.11, f32[]{:T(128)} %constant.16.clone.1), dimensions={0}, to_apply=%region_3.0 | reduce | flops 16252928 | bytes 69206016 | tf_op jit(solution)/shard_map/reduce_sum | solution.py:43
  881.4 5.9 convolution_add_fusion
  (3 shorter events, 0.0 us)
Async XLA Ops:
  7.2 1.6 copy-start
  7.2 341.3 %all-reduce.3.cloned.1.call-start = ((), (), s32[]{:S(2)}) async-start(), calls=%async_computation | async-start | bytes 16777216 | tf_op jit(solution)/shard_map/psum | solution.py:26
  13.9 1.3 copy-start.1
  21.3 453.2 %all-reduce.5.cloned.1.call-start = ((), (), s32[]{:S(2)}) async-start(), calls=%async_computation.1 | async-start | bytes 4194304 | tf_op jit(solution)/shard_map/psum | solution.py:34
  366.5 492.6 %all-gather.3.cloned.1.call-start = ((), (), s32[]{:S(2)}) async-start(), calls=%async_computation.2 | async-start | bytes 69206016 | tf_op jit(solution)/shard_map/all_gather | solution.py:43
Sparse Core Ops, SparseCore 0:
  21.5 326.9 all-reduce.2
  366.6 107.8 all-reduce.4
  482.1 377.0 all-gather.2
